TPU v7x, 32 devices: a whole 2x2x4 slice. The times are simulated.
32 devices in a mesh: blk: 8 (over z, core), uly: 4 (over y, x).
Axes of the slice: x: 2, y: 2, z: 4, core: 2. Of those that a mesh axis runs over, the one named last changes fastest.
Arguments:
- queries: bfloat16 [1024, 128, 128], P(('blk', 'uly')), may hold values from -8 to 8
- query_tangents: bfloat16 [1024, 128, 4, 128], P(('blk', 'uly')), may hold values from -6 to 6
- keys: bfloat16 [1024, 8, 128], P(('blk', 'uly')), may hold values from -8 to 8
- key_tangents: bfloat16 [1024, 8, 4, 128], P(('blk', 'uly')), may hold values from -6 to 6
- values: bfloat16 [1024, 8, 128], P(('blk', 'uly')), may hold values from -6 to 6
- value_tangents: bfloat16 [1024, 8, 4, 128], P(('blk', 'uly')), may hold values from -6 to 6
- span_order: int32 [16], replicated, may hold values from 0 to 15, as said below
Outputs:
- attention_out: bfloat16 [1024, 128, 128], P(('blk', 'uly'))
- tangent_out: bfloat16 [1024, 128, 4, 128], P(('blk', 'uly'))
Inputs may be any that keep to these rules, and one draw needn't show every extreme that they name: span_order is a permutation of the span positions; for every b the stored spans 2 * b and 2 * b + 1 hold positions c and 15 - c for some c.
All inputs are finite; a program needn't handle non-finite values.
Results may differ from a plain program's by a relative error of at most 0.0055.
Values may be sent and summed in bfloat16 or wider, within the bound.
A program may use at most 128 MiB of HBM per device.

v0:
```python
import jax
import jax.numpy as jnp
from jax import lax
from jax.sharding import PartitionSpec as P

HQ = 128
KVH = 8


def positions(stored, span_order, span_rows):
    span_ids = stored // span_rows
    table_ids = jnp.arange(span_order.shape[0], dtype=jnp.int32)
    looked_up = jnp.sum(
        jnp.where(span_ids[:, None] == table_ids[None, :], span_order[None, :], 0), axis=1
    )
    return looked_up * span_rows + stored % span_rows


def per_device(queries, query_tangents, keys, key_tangents, values, value_tangents, span_order):
    local_queries, local_tangents = (
        lax.all_to_all(queries, "uly", split_axis=1, concat_axis=0, tiled=True),
        lax.all_to_all(query_tangents, "uly", split_axis=1, concat_axis=0, tiled=True),
    )
    query_rows = local_queries.shape[0]
    span_rows = query_rows // 2
    head_size = local_queries.shape[2]
    group = HQ // KVH
    kv_local = local_queries.shape[1] // group
    probes = local_tangents.shape[2]
    scaling = head_size ** (-0.5)
    stored = lax.axis_index("blk") * query_rows + jnp.arange(query_rows, dtype=jnp.int32)
    query_places = positions(stored, span_order, span_rows)
    latest = jnp.max(query_places)
    query_heads = jnp.transpose(
        local_queries.reshape(query_rows, kv_local, group, head_size), (1, 2, 0, 3)
    )
    tangent_heads = jnp.transpose(
        local_tangents.reshape(query_rows, kv_local, group, probes, head_size), (1, 2, 3, 0, 4)
    )

    def update(carry, block):
        key_block, key_tan, value_block, value_tan, key_places = block
        running_max, totals, primal_sums, tangent_sums, shifts = carry
        visible = key_places[None, :] <= query_places[:, None]
        scores = (
            jnp.einsum("grqd,kgd->grqk", query_heads, key_block, preferred_element_type=jnp.float32)
            * scaling
        )
        scores = jnp.where(visible[None, None], scores, -1e30)
        new_max = jnp.maximum(running_max, jnp.max(scores, axis=-1))
        rescale = jnp.exp(running_max - new_max)
        weights_full = jnp.where(visible[None, None], jnp.exp(scores - new_max[..., None]), 0.0)
        weights_half = weights_full.astype(jnp.bfloat16)
        score_tan = jnp.einsum(
            "grpqd,kgd->grpqk", tangent_heads, key_block, preferred_element_type=jnp.float32
        )
        score_tan = score_tan + jnp.einsum(
            "grqd,kgpd->grpqk", query_heads, key_tan, preferred_element_type=jnp.float32
        )
        weighted = weights_full[:, :, None] * (score_tan * scaling)
        totals = totals * rescale + jnp.sum(weights_full, axis=-1)
        primal_sums = primal_sums * rescale[..., None] + jnp.einsum(
            "grqk,kgd->grqd", weights_half, value_block, preferred_element_type=jnp.float32
        )
        shifts = shifts * rescale[:, :, None] + jnp.sum(weighted, axis=-1)
        tangent_sums = tangent_sums * rescale[:, :, None, :, None]
        tangent_sums = tangent_sums + jnp.einsum(
            "grpqk,kgd->grpqd",
            weighted.astype(jnp.bfloat16),
            value_block,
            preferred_element_type=jnp.float32,
        )
        tangent_sums = tangent_sums + jnp.einsum(
            "grqk,kgpd->grpqd", weights_half, value_tan, preferred_element_type=jnp.float32
        )
        return (new_max, totals, primal_sums, tangent_sums, shifts)

    def keep_state(carry, block):
        return carry

    def visit(carry, block):
        reachable = jnp.min(block[4]) <= latest
        return (lax.cond(reachable, update, keep_state, carry, block), None)

    initial = (
        jnp.full((kv_local, group, query_rows), -1e30, jnp.float32),
        jnp.zeros((kv_local, group, query_rows), jnp.float32),
        jnp.zeros((kv_local, group, query_rows, head_size), jnp.float32),
        jnp.zeros((kv_local, group, probes, query_rows, head_size), jnp.float32),
        jnp.zeros((kv_local, group, probes, query_rows), jnp.float32),
    )
    head_keys, head_key_tan, head_values, head_value_tan = (
        lax.all_to_all(keys, "uly", split_axis=1, concat_axis=0, tiled=True),
        lax.all_to_all(key_tangents, "uly", split_axis=1, concat_axis=0, tiled=True),
        lax.all_to_all(values, "uly", split_axis=1, concat_axis=0, tiled=True),
        lax.all_to_all(value_tangents, "uly", split_axis=1, concat_axis=0, tiled=True),
    )
    carry = initial
    key_piece = lax.all_gather(head_keys, "blk", axis=0, tiled=True)
    key_tan_piece = lax.all_gather(head_key_tan, "blk", axis=0, tiled=True)
    value_piece = lax.all_gather(head_values, "blk", axis=0, tiled=True)
    value_tan_piece = lax.all_gather(head_value_tan, "blk", axis=0, tiled=True)
    piece_rows = key_piece.shape[0]
    block_rows = 256
    block_total = piece_rows // block_rows
    places = positions(jnp.arange(piece_rows, dtype=jnp.int32), span_order, span_rows)
    stacked = (
        key_piece.reshape(block_total, block_rows, kv_local, head_size),
        key_tan_piece.reshape(block_total, block_rows, kv_local, probes, head_size),
        value_piece.reshape(block_total, block_rows, kv_local, head_size),
        value_tan_piece.reshape(block_total, block_rows, kv_local, probes, head_size),
        places.reshape(block_total, block_rows),
    )
    carry, unused = lax.scan(visit, carry, stacked)
    running_max, totals, primal_sums, tangent_sums, shifts = carry
    primal = primal_sums / totals[..., None]
    tangent = (
        tangent_sums / totals[:, :, None, :, None]
        - primal[:, :, None] * (shifts / totals[:, :, None])[..., None]
    )
    output_rows = jnp.transpose(primal.astype(jnp.bfloat16), (2, 0, 1, 3)).reshape(
        query_rows, kv_local * group, head_size
    )
    tangent_rows = jnp.transpose(tangent.astype(jnp.bfloat16), (3, 0, 1, 2, 4)).reshape(
        query_rows, kv_local * group, probes, head_size
    )
    attention_out, tangent_out = (
        lax.all_to_all(output_rows, "uly", split_axis=0, concat_axis=1, tiled=True),
        lax.all_to_all(tangent_rows, "uly", split_axis=0, concat_axis=1, tiled=True),
    )
    return (attention_out, tangent_out)


def solution(mesh):
    placed = (
        P(("blk", "uly"), None, None),
        P(("blk", "uly"), None, None, None),
        P(("blk", "uly"), None, None),
        P(("blk", "uly"), None, None, None),
        P(("blk", "uly"), None, None),
        P(("blk", "uly"), None, None, None),
        P(),
    )
    return jax.shard_map(
        per_device,
        mesh=mesh,
        in_specs=placed,
        out_specs=(P(("blk", "uly"), None, None), P(("blk", "uly"), None, None, None)),
        check_vma=False,
    )
```

profile of v0, /device:TPU:0, one launch (start us, length us, event | category | flops | bytes accessed | tf_op | source)
XLA Modules:
  0.0 424.2 jit_solution(10656126634466372391)
XLA Ops:
  8.3 10.7 %all_to_all.138 = bf16[32,8,4,128]{3,0,2,1:T(8,128)(2,1)S(1)} all-to-all(bf16[32,8,4,128]{3,0,2,1:T(8,128)(2,1)S(1)} %copy.84), channel_id=1, replica_groups=mesh['blk'=8,'uly'=4] {'uly'}, dimensions={1} | all-to-all | bytes 524288 | tf_op jit(solution)/shard_map/all_to_all | solution.py:94
  21.2 3.3 all-to-all-start
  26.0 3.3 all-to-all-done
  29.3 3.3 all-to-all-start.2
  34.4 3.1 all-to-all-done.2
  37.4 3.4 all-to-all-start.5
  40.9 2.9 copy.78
  46.2 3.5 all-to-all-start.1
  50.6 6.6 %copy.82 = bf16[32,128,4,128]{3,2,0,1:T(4,128)(2,1)} copy(bf16[32,128,4,128]{3,2,1,0:T(4,128)(2,1)} %param.12) | data formatting | bytes 8388608 | tf_op args[1]
  59.7 4.9 %all-to-all-start.3 = ((bf16[32,128,4,128]{3,2,0,1:T(4,128)(2,1)}), bf16[32,128,4,128]{3,2,0,1:T(4,128)(2,1)}, u32[]{:S(2)}, u32[]{:S(2)}) async-start(bf16[32,128,4,128]{3,2,0,1:T(4,128)(2,1)} %copy.82), calls=%async_computation.3 | async-start | bytes 8388608 | tf_op jit(solution)/shard_map/all_to_all | solution.py:22
  65.5 17.9 %all_gather.12 = bf16[1024,2,128]{2,0,1:T(8,128)(2,1)S(1)} all-gather(bf16[128,2,128]{2,0,1:T(8,128)(2,1)S(1)} %bitcast.140), channel_id=1, replica_groups=mesh['blk'=8,'uly'=4] {'blk'}, dimensions={0}, use_global_device_ids=true | all-gather | bytes 589824 | tf_op jit(solution)/shard_map/all_gather | solution.py:99
  84.2 14.7 %all_gather.13 = bf16[1024,2,128]{2,0,1:T(8,128)(2,1)S(1)} all-gather(bf16[128,2,128]{2,0,1:T(8,128)(2,1)S(1)} %bitcast.141), channel_id=1, replica_groups=mesh['blk'=8,'uly'=4] {'blk'}, dimensions={0}, use_global_device_ids=true | all-gather | bytes 589824 | tf_op jit(solution)/shard_map/all_gather | solution.py:101
  99.9 7.5 %all-to-all-done.3 = bf16[32,128,4,128]{3,2,0,1:T(4,128)(2,1)} async-done(((bf16[32,128,4,128]{3,2,0,1:T(4,128)(2,1)}), bf16[32,128,4,128]{3,2,0,1:T(4,128)(2,1)}, u32[]{:S(2)}, u32[]{:S(2)}) %all-to-all-start.3) | async-done | bytes 4194336 | tf_op jit(solution)/shard_map/all_to_all | solution.py:22
  107.4 5.4 %copy.83 = bf16[4,32,32,4,128]{4,1,0,3,2:T(8,128)(2,1)} copy(bf16[4,32,32,4,128]{4,3,1,2,0:T(4,128)(2,1)} %bitcast.37) | data formatting | bytes 8388608 | tf_op jit(solution)/shard_map/all_to_all | solution.py:22
  112.8 3.1 copy.90
  117.6 4.3 %broadcast_in_dim.87 = f32[2,16,4,128,128]{4,3,2,1,0:T(8,128)} broadcast(f32[]{:T(128)} %constant.103.clone.1), dimensions={} | broadcast | bytes 8388612 | tf_op jit(solution)/shard_map/broadcast_in_dim | solution.py:89
  123.5 212.6 %while.18 = (s32[]{:T(128)}, f32[2,16,128]{2,1,0:T(8,128)S(1)}, f32[2,16,128]{2,1,0:T(8,128)S(1)}, f32[2,16,128,128]{3,2,1,0:T(8,128)}, f32[2,16,4,128,128]{4,3,...) while((s32[]{:T(128)}, f32[2,16,128]{2,1,0:T(8,128)S(1)}, ...), condition=%wide.region_10.11_spmd, body=%wide.region_3.10_spmd.sunk | while | flops 4875936256 | bytes 138631600 | solution.py:114
  125.7 51.1 %conditional.2 = ((f32[2,16,128]{2,1,0:T(8,128)S(1)}, f32[2,16,128]{2,1,0:T(8,128)S(1)}, f32[2,16,128,128]{3,2,1,0:T(8,128)}, f32[2,16,4,128,128]{4,3,2,1,0:T(8,128)}, f32[2,16,4,128]{3,2,1,0:T(4,128)S(1)})) conditional(s32[]{:T(128)} %convert_element_type.33, (f32[2,16,128]{2,1,0:T(8,128)S(1)}, f32[2,16,128]{2,1,0:T(8,128)S(1)}, ...), branch_computations={%region_5.5_spmd, %region_6.9_spmd} | conditional | flops 4875935744 | bytes 138629216 | solution.py:83
  127.5 3.3 broadcast_multiply_fusion
  130.8 9.1 %fusion.7 = f32[2,256,4,16,128]{4,1,2,3,0:T(8,128)} fusion(bf16[2,16,128,128]{3,2,1,0:T(8,128)(2,1)S(1)} %get-tuple-element.183, bf16[4,256,2,4,128]{4,1,3,2,0:T(8,128)(2,1)} %get-tuple-element.189, s32[]{:T(128)} %get-tuple-element.182), kind=kOutput, calls=%fused_computation.13 | convolution fusion | flops 1073741824 | bytes 18350592 | tf_op jit(solution)/shard_map/while/body/eval_jaxpr/cond/branch_1_fun/grqd,kgpd->grpqk/dot_general | solution.py:57
  139.9 13.2 %fusion.40 = (f32[2,16,4,128]{3,2,1,0:T(4,128)S(1)}, bf16[2,16,4,128,256]{3,4,2,1,0:T(8,128)(2,1)}) fusion(f32[2,16,128,256]{2,3,1,0:T(8,128)} %get-tuple-element.327, f32[2,256,4,16,128]{4,1,2,3,0:T(8,128)} %fusion.7, bf16[2,16,4,128,128]{4,3,2,1,0:T(8,128)(2,1)} %get-tuple-element.188, bf16[4,256,2,128]{3,1,2,0:T(8,128)(2,1)} %get-tuple-element.181, ...), kind=kOutput, calls=%fused_computation.70 | convolution fusion | flops 1090502656 | bytes 33751552 | tf_op jit(solution)/shard_map/while/body/eval_jaxpr/cond/branch_1_fun/grpqd,kgd->grpqk/dot_general | solution.py:54
  153.1 10.0 %fusion.1 = f32[2,16,4,128,128]{4,3,2,1,0:T(8,128)} fusion(bf16[2,16,4,128,256]{3,4,2,1,0:T(8,128)(2,1)} %get-tuple-element.332, bf16[4,256,2,128]{3,1,2,0:T(8,128)(2,1)} %get-tuple-element.186, s32[]{:T(128)} %get-tuple-element.182), kind=kOutput, calls=%fused_computation.3 | convolution fusion | flops 1073741824 | bytes 16908800 | tf_op jit(solution)/shard_map/while/body/eval_jaxpr/cond/branch_1_fun/grpqk,kgd->grpqd/dot_general | solution.py:67
  163.2 9.5 %bitcast_add_fusion.1 = f32[2,16,4,128,128]{4,3,2,1,0:T(8,128)} fusion(f32[2,16,4,128,128]{4,3,2,1,0:T(8,128)} %fusion.1, f32[2,16,4,128,128]{4,3,2,1,0:T(8,128)} %get-tuple-element.187, f32[2,16,128]{2,1,0:T(8,128)S(1)} %get-tuple-element.320, bf16[4,256,2,4,128]{4,1,3,2,0:T(8,128)(2,1)S(1)} %get-tuple-element.190, s32[]{:T(128)} %get-tuple-element.182, ...), kind=kOutput, calls=%fused_computation.2 | convolution fusion | flops 1085276160 | bytes 29949956 | tf_op jit(solution)/shard_map/while/body/eval_jaxpr/cond/branch_1_fun/grqk,kgpd->grpqd/dot_general | solution.py:73
  178.8 51.1 %conditional.2 = ((f32[2,16,128]{2,1,0:T(8,128)S(1)}, f32[2,16,128]{2,1,0:T(8,128)S(1)}, f32[2,16,128,128]{3,2,1,0:T(8,128)}, f32[2,16,4,128,128]{4,3,2,1,0:T(8,128)}, f32[2,16,4,128]{3,2,1,0:T(4,128)S(1)})) conditional(s32[]{:T(128)} %convert_element_type.33, (f32[2,16,128]{2,1,0:T(8,128)S(1)}, f32[2,16,128]{2,1,0:T(8,128)S(1)}, ...), branch_computations={%region_5.5_spmd, %region_6.9_spmd} | conditional | flops 4875935744 | bytes 138629216 | solution.py:83
  180.6 3.3 broadcast_multiply_fusion
  183.9 9.1 %fusion.7 = f32[2,256,4,16,128]{4,1,2,3,0:T(8,128)} fusion(bf16[2,16,128,128]{3,2,1,0:T(8,128)(2,1)S(1)} %get-tuple-element.183, bf16[4,256,2,4,128]{4,1,3,2,0:T(8,128)(2,1)} %get-tuple-element.189, s32[]{:T(128)} %get-tuple-element.182), kind=kOutput, calls=%fused_computation.13 | convolution fusion | flops 1073741824 | bytes 18350592 | tf_op jit(solution)/shard_map/while/body/eval_jaxpr/cond/branch_1_fun/grqd,kgpd->grpqk/dot_general | solution.py:57
  193.0 13.2 %fusion.40 = (f32[2,16,4,128]{3,2,1,0:T(4,128)S(1)}, bf16[2,16,4,128,256]{3,4,2,1,0:T(8,128)(2,1)}) fusion(f32[2,16,128,256]{2,3,1,0:T(8,128)} %get-tuple-element.327, f32[2,256,4,16,128]{4,1,2,3,0:T(8,128)} %fusion.7, bf16[2,16,4,128,128]{4,3,2,1,0:T(8,128)(2,1)} %get-tuple-element.188, bf16[4,256,2,128]{3,1,2,0:T(8,128)(2,1)} %get-tuple-element.181, ...), kind=kOutput, calls=%fused_computation.70 | convolution fusion | flops 1090502656 | bytes 33751552 | tf_op jit(solution)/shard_map/while/body/eval_jaxpr/cond/branch_1_fun/grpqd,kgd->grpqk/dot_general | solution.py:54
  206.3 10.0 %fusion.1 = f32[2,16,4,128,128]{4,3,2,1,0:T(8,128)} fusion(bf16[2,16,4,128,256]{3,4,2,1,0:T(8,128)(2,1)} %get-tuple-element.332, bf16[4,256,2,128]{3,1,2,0:T(8,128)(2,1)} %get-tuple-element.186, s32[]{:T(128)} %get-tuple-element.182), kind=kOutput, calls=%fused_computation.3 | convolution fusion | flops 1073741824 | bytes 16908800 | tf_op jit(solution)/shard_map/while/body/eval_jaxpr/cond/branch_1_fun/grpqk,kgd->grpqd/dot_general | solution.py:67
  216.3 9.5 %bitcast_add_fusion.1 = f32[2,16,4,128,128]{4,3,2,1,0:T(8,128)} fusion(f32[2,16,4,128,128]{4,3,2,1,0:T(8,128)} %fusion.1, f32[2,16,4,128,128]{4,3,2,1,0:T(8,128)} %get-tuple-element.187, f32[2,16,128]{2,1,0:T(8,128)S(1)} %get-tuple-element.320, bf16[4,256,2,4,128]{4,1,3,2,0:T(8,128)(2,1)S(1)} %get-tuple-element.190, s32[]{:T(128)} %get-tuple-element.182, ...), kind=kOutput, calls=%fused_computation.2 | convolution fusion | flops 1085276160 | bytes 29949956 | tf_op jit(solution)/shard_map/while/body/eval_jaxpr/cond/branch_1_fun/grqk,kgpd->grpqd/dot_general | solution.py:73
  231.9 51.1 %conditional.2 = ((f32[2,16,128]{2,1,0:T(8,128)S(1)}, f32[2,16,128]{2,1,0:T(8,128)S(1)}, f32[2,16,128,128]{3,2,1,0:T(8,128)}, f32[2,16,4,128,128]{4,3,2,1,0:T(8,128)}, f32[2,16,4,128]{3,2,1,0:T(4,128)S(1)})) conditional(s32[]{:T(128)} %convert_element_type.33, (f32[2,16,128]{2,1,0:T(8,128)S(1)}, f32[2,16,128]{2,1,0:T(8,128)S(1)}, ...), branch_computations={%region_5.5_spmd, %region_6.9_spmd} | conditional | flops 4875935744 | bytes 138629216 | solution.py:83
  233.7 3.3 broadcast_multiply_fusion
  237.0 9.1 %fusion.7 = f32[2,256,4,16,128]{4,1,2,3,0:T(8,128)} fusion(bf16[2,16,128,128]{3,2,1,0:T(8,128)(2,1)S(1)} %get-tuple-element.183, bf16[4,256,2,4,128]{4,1,3,2,0:T(8,128)(2,1)} %get-tuple-element.189, s32[]{:T(128)} %get-tuple-element.182), kind=kOutput, calls=%fused_computation.13 | convolution fusion | flops 1073741824 | bytes 18350592 | tf_op jit(solution)/shard_map/while/body/eval_jaxpr/cond/branch_1_fun/grqd,kgpd->grpqk/dot_general | solution.py:57
  246.1 13.2 %fusion.40 = (f32[2,16,4,128]{3,2,1,0:T(4,128)S(1)}, bf16[2,16,4,128,256]{3,4,2,1,0:T(8,128)(2,1)}) fusion(f32[2,16,128,256]{2,3,1,0:T(8,128)} %get-tuple-element.327, f32[2,256,4,16,128]{4,1,2,3,0:T(8,128)} %fusion.7, bf16[2,16,4,128,128]{4,3,2,1,0:T(8,128)(2,1)} %get-tuple-element.188, bf16[4,256,2,128]{3,1,2,0:T(8,128)(2,1)} %get-tuple-element.181, ...), kind=kOutput, calls=%fused_computation.70 | convolution fusion | flops 1090502656 | bytes 33751552 | tf_op jit(solution)/shard_map/while/body/eval_jaxpr/cond/branch_1_fun/grpqd,kgd->grpqk/dot_general | solution.py:54
  259.4 10.0 %fusion.1 = f32[2,16,4,128,128]{4,3,2,1,0:T(8,128)} fusion(bf16[2,16,4,128,256]{3,4,2,1,0:T(8,128)(2,1)} %get-tuple-element.332, bf16[4,256,2,128]{3,1,2,0:T(8,128)(2,1)} %get-tuple-element.186, s32[]{:T(128)} %get-tuple-element.182), kind=kOutput, calls=%fused_computation.3 | convolution fusion | flops 1073741824 | bytes 16908800 | tf_op jit(solution)/shard_map/while/body/eval_jaxpr/cond/branch_1_fun/grpqk,kgd->grpqd/dot_general | solution.py:67
  269.4 9.5 %bitcast_add_fusion.1 = f32[2,16,4,128,128]{4,3,2,1,0:T(8,128)} fusion(f32[2,16,4,128,128]{4,3,2,1,0:T(8,128)} %fusion.1, f32[2,16,4,128,128]{4,3,2,1,0:T(8,128)} %get-tuple-element.187, f32[2,16,128]{2,1,0:T(8,128)S(1)} %get-tuple-element.320, bf16[4,256,2,4,128]{4,1,3,2,0:T(8,128)(2,1)S(1)} %get-tuple-element.190, s32[]{:T(128)} %get-tuple-element.182, ...), kind=kOutput, calls=%fused_computation.2 | convolution fusion | flops 1085276160 | bytes 29949956 | tf_op jit(solution)/shard_map/while/body/eval_jaxpr/cond/branch_1_fun/grqk,kgpd->grpqd/dot_general | solution.py:73
  285.0 51.1 %conditional.2 = ((f32[2,16,128]{2,1,0:T(8,128)S(1)}, f32[2,16,128]{2,1,0:T(8,128)S(1)}, f32[2,16,128,128]{3,2,1,0:T(8,128)}, f32[2,16,4,128,128]{4,3,2,1,0:T(8,128)}, f32[2,16,4,128]{3,2,1,0:T(4,128)S(1)})) conditional(s32[]{:T(128)} %convert_element_type.33, (f32[2,16,128]{2,1,0:T(8,128)S(1)}, f32[2,16,128]{2,1,0:T(8,128)S(1)}, ...), branch_computations={%region_5.5_spmd, %region_6.9_spmd} | conditional | flops 4875935744 | bytes 138629216 | solution.py:83
  286.8 3.3 broadcast_multiply_fusion
  290.1 9.1 %fusion.7 = f32[2,256,4,16,128]{4,1,2,3,0:T(8,128)} fusion(bf16[2,16,128,128]{3,2,1,0:T(8,128)(2,1)S(1)} %get-tuple-element.183, bf16[4,256,2,4,128]{4,1,3,2,0:T(8,128)(2,1)} %get-tuple-element.189, s32[]{:T(128)} %get-tuple-element.182), kind=kOutput, calls=%fused_computation.13 | convolution fusion | flops 1073741824 | bytes 18350592 | tf_op jit(solution)/shard_map/while/body/eval_jaxpr/cond/branch_1_fun/grqd,kgpd->grpqk/dot_general | solution.py:57
  299.2 13.2 %fusion.40 = (f32[2,16,4,128]{3,2,1,0:T(4,128)S(1)}, bf16[2,16,4,128,256]{3,4,2,1,0:T(8,128)(2,1)}) fusion(f32[2,16,128,256]{2,3,1,0:T(8,128)} %get-tuple-element.327, f32[2,256,4,16,128]{4,1,2,3,0:T(8,128)} %fusion.7, bf16[2,16,4,128,128]{4,3,2,1,0:T(8,128)(2,1)} %get-tuple-element.188, bf16[4,256,2,128]{3,1,2,0:T(8,128)(2,1)} %get-tuple-element.181, ...), kind=kOutput, calls=%fused_computation.70 | convolution fusion | flops 1090502656 | bytes 33751552 | tf_op jit(solution)/shard_map/while/body/eval_jaxpr/cond/branch_1_fun/grpqd,kgd->grpqk/dot_general | solution.py:54
  312.5 10.0 %fusion.1 = f32[2,16,4,128,128]{4,3,2,1,0:T(8,128)} fusion(bf16[2,16,4,128,256]{3,4,2,1,0:T(8,128)(2,1)} %get-tuple-element.332, bf16[4,256,2,128]{3,1,2,0:T(8,128)(2,1)} %get-tuple-element.186, s32[]{:T(128)} %get-tuple-element.182), kind=kOutput, calls=%fused_computation.3 | convolution fusion | flops 1073741824 | bytes 16908800 | tf_op jit(solution)/shard_map/while/body/eval_jaxpr/cond/branch_1_fun/grpqk,kgd->grpqd/dot_general | solution.py:67
  322.5 9.5 %bitcast_add_fusion.1 = f32[2,16,4,128,128]{4,3,2,1,0:T(8,128)} fusion(f32[2,16,4,128,128]{4,3,2,1,0:T(8,128)} %fusion.1, f32[2,16,4,128,128]{4,3,2,1,0:T(8,128)} %get-tuple-element.187, f32[2,16,128]{2,1,0:T(8,128)S(1)} %get-tuple-element.320, bf16[4,256,2,4,128]{4,1,3,2,0:T(8,128)(2,1)S(1)} %get-tuple-element.190, s32[]{:T(128)} %get-tuple-element.182, ...), kind=kOutput, calls=%fused_computation.2 | convolution fusion | flops 1085276160 | bytes 29949956 | tf_op jit(solution)/shard_map/while/body/eval_jaxpr/cond/branch_1_fun/grqk,kgpd->grpqd/dot_general | solution.py:73
  339.8 3.5 all-to-all-start.6
  343.3 5.6 %fusion.30 = bf16[128,2,16,4,128]{4,0,3,2,1:T(8,128)(2,1)S(1)} fusion(f32[2,16,4,128]{3,2,1,0:T(4,128)S(1)} %broadcast_divide_fusion.1, f32[2,16,128,128]{3,2,1,0:T(8,128)S(1)} %get-tuple-element.324, f32[2,16,4,128,128]{4,3,2,1,0:T(8,128)} %get-tuple-element.221, f32[2,16,128]{2,1,0:T(8,128)S(1)} %get-tuple-element.220), kind=kLoop, calls=%fused_computation.40 | loop fusion | flops 8388608 | bytes 14761984 | tf_op jit(solution)/shard_map/transpose | solution.py:124
  348.9 4.7 %copy.94 = bf16[128,2,16,4,128]{4,2,1,3,0:T(8,128)(2,1)} copy(bf16[128,2,16,4,128]{4,0,3,2,1:T(8,128)(2,1)S(1)} %fusion.30) | data formatting | bytes 8388608 | tf_op jit(solution)/shard_map/transpose | solution.py:124
  356.4 4.8 %all-to-all-start.7 = ((bf16[128,32,4,128]{3,1,2,0:T(8,128)(2,1)}), bf16[128,32,4,128]{3,1,2,0:T(8,128)(2,1)}, u32[]{:S(2)}, u32[]{:S(2)}) async-start(bf16[128,32,4,128]{3,1,2,0:T(8,128)(2,1)} %bitcast.126), calls=%async_computation.7 | async-start | bytes 8388608 | tf_op jit(solution)/shard_map/all_to_all | solution.py:129
  362.4 45.8 %all-to-all-done.7 = bf16[128,32,4,128]{3,1,2,0:T(8,128)(2,1)} async-done(((bf16[128,32,4,128]{3,1,2,0:T(8,128)(2,1)}), bf16[128,32,4,128]{3,1,2,0:T(8,128)(2,1)}, u32[]{:S(2)}, u32[]{:S(2)}) %all-to-all-start.7) | async-done | bytes 4194336 | tf_op jit(solution)/shard_map/all_to_all | solution.py:129
  408.2 3.3 copy.95
  411.4 5.9 %copy.96 = bf16[32,128,4,128]{3,2,1,0:T(4,128)(2,1)} copy(bf16[32,128,4,128]{3,1,2,0:T(8,128)(2,1)S(1)} %bitcast.127) | data formatting | bytes 8388608
  (87 shorter events, 52.1 us)
Async XLA Ops:
  7.2 105.6 %all-gather.3.cloned.1.call-start = ((), (), s32[]{:S(2)}) async-start(), calls=%async_computation.8 | async-start | bytes 2359296 | tf_op jit(solution)/shard_map/all_gather | solution.py:100
  21.2 8.1 %all-to-all-start = ((bf16[32,8,128]{2,0,1:T(8,128)(2,1)}), bf16[32,8,128]{2,0,1:T(8,128)(2,1)S(1)}, u32[]{:S(2)}, u32[]{:S(2)}) async-start(bf16[32,8,128]{2,0,1:T(8,128)(2,1)} %copy.76), calls=%async_computation | async-start | bytes 131072 | tf_op jit(solution)/shard_map/all_to_all | solution.py:93
  29.3 8.1 %all-to-all-start.2 = ((bf16[32,8,128]{2,0,1:T(8,128)(2,1)}), bf16[32,8,128]{2,0,1:T(8,128)(2,1)S(1)}, u32[]{:S(2)}, u32[]{:S(2)}) async-start(bf16[32,8,128]{2,0,1:T(8,128)(2,1)} %copy.80), calls=%async_computation.2 | async-start | bytes 131072 | tf_op jit(solution)/shard_map/all_to_all | solution.py:95
  37.4 8.8 %all-to-all-start.5 = ((bf16[32,8,4,128]{3,0,2,1:T(8,128)(2,1)}), bf16[32,8,4,128]{3,0,2,1:T(8,128)(2,1)S(1)}, u32[]{:S(2)}, u32[]{:S(2)}) async-start(bf16[32,8,4,128]{3,0,2,1:T(8,128)(2,1)} %copy.86), calls=%async_computation.5 | async-start | bytes 524288 | tf_op jit(solution)/shard_map/all_to_all | solution.py:96
  46.2 13.5 %all-to-all-start.1 = ((bf16[32,128,128]{2,0,1:T(8,128)(2,1)}), bf16[32,128,128]{2,0,1:T(8,128)(2,1)S(1)}, u32[]{:S(2)}, u32[]{:S(2)}) async-start(bf16[32,128,128]{2,0,1:T(8,128)(2,1)} %copy.78), calls=%async_computation.1 | async-start | bytes 2097152 | tf_op jit(solution)/shard_map/all_to_all | solution.py:21
  49.7 66.2 %all-gather.5.cloned.1.call-start = ((), (), s32[]{:S(2)}) async-start(), calls=%async_computation.9 | async-start | bytes 2359296 | tf_op jit(solution)/shard_map/all_gather | solution.py:102
  57.1 7.4 %copy-start.2 = (s32[16]{0:T(128)S(1)}, s32[16]{0:T(128)}, u32[]{:S(2)}) copy-start(s32[16]{0:T(128)} %param.17) | copy-start | bytes 196
  59.7 47.7 %all-to-all-start.3 = ((bf16[32,128,4,128]{3,2,0,1:T(4,128)(2,1)}), bf16[32,128,4,128]{3,2,0,1:T(4,128)(2,1)}, u32[]{:S(2)}, u32[]{:S(2)}) async-start(bf16[32,128,4,128]{3,2,0,1:T(4,128)(2,1)} %copy.82), calls=%async_computation.3 | async-start | bytes 8388608 | tf_op jit(solution)/shard_map/all_to_all | solution.py:22
  163.1 9.6 %copy-start = (f32[2,16,128,128]{3,2,1,0:T(8,128)S(1)}, f32[2,16,128,128]{3,2,1,0:T(8,128)}, u32[]{:S(2)}) copy-start(f32[2,16,128,128]{3,2,1,0:T(8,128)} %get-tuple-element.185) | copy-start | bytes 6291460 | tf_op jit(solution)/shard_map/while/body/eval_jaxpr/cond
  175.5 1.3 copy-start.1
  216.2 9.6 %copy-start = (f32[2,16,128,128]{3,2,1,0:T(8,128)S(1)}, f32[2,16,128,128]{3,2,1,0:T(8,128)}, u32[]{:S(2)}) copy-start(f32[2,16,128,128]{3,2,1,0:T(8,128)} %get-tuple-element.185) | copy-start | bytes 6291460 | tf_op jit(solution)/shard_map/while/body/eval_jaxpr/cond
  228.6 1.3 copy-start.1
  269.4 9.6 %copy-start = (f32[2,16,128,128]{3,2,1,0:T(8,128)S(1)}, f32[2,16,128,128]{3,2,1,0:T(8,128)}, u32[]{:S(2)}) copy-start(f32[2,16,128,128]{3,2,1,0:T(8,128)} %get-tuple-element.185) | copy-start | bytes 6291460 | tf_op jit(solution)/shard_map/while/body/eval_jaxpr/cond
  281.7 1.3 copy-start.1
  322.5 9.6 %copy-start = (f32[2,16,128,128]{3,2,1,0:T(8,128)S(1)}, f32[2,16,128,128]{3,2,1,0:T(8,128)}, u32[]{:S(2)}) copy-start(f32[2,16,128,128]{3,2,1,0:T(8,128)} %get-tuple-element.185) | copy-start | bytes 6291460 | tf_op jit(solution)/shard_map/while/body/eval_jaxpr/cond
  334.8 1.3 copy-start.1
  339.8 16.6 %all-to-all-start.6 = ((bf16[128,32,128]{2,1,0:T(8,128)(2,1)}), bf16[128,32,128]{2,1,0:T(8,128)(2,1)S(1)}, u32[]{:S(2)}, u32[]{:S(2)}) async-start(bf16[128,32,128]{2,1,0:T(8,128)(2,1)} %bitcast.130), calls=%async_computation.6 | async-start | bytes 2097152 | tf_op jit(solution)/shard_map/all_to_all | solution.py:128
  356.4 51.8 %all-to-all-start.7 = ((bf16[128,32,4,128]{3,1,2,0:T(8,128)(2,1)}), bf16[128,32,4,128]{3,1,2,0:T(8,128)(2,1)}, u32[]{:S(2)}, u32[]{:S(2)}) async-start(bf16[128,32,4,128]{3,1,2,0:T(8,128)(2,1)} %bitcast.126), calls=%async_computation.7 | async-start | bytes 8388608 | tf_op jit(solution)/shard_map/all_to_all | solution.py:129
Sparse Core Ops, SparseCore 0:
  19.9 28.8 all-gather.2
  52.2 35.0 all-gather.4
where the time goes:
time: 426 us; the launch traced here: 424 us
  matrix products  185 us (43%)
  waiting for transfers between devices  67.5 us (16%)
  local copies, waits for them, and re-layouts  56.6 us (13%)
  blocking collectives  43.3 us (10%)
  starting transfers between devices  26.8 us (6%)
  other arithmetic  25.2 us (6%)
  between operations  14.2 us (3%)
  loops' own time  5.56 us (1%)
    dot_general x4, matrix products, update(): jnp.einsum('grpqd,kgd->grpqk', tangent_heads, key_block, preferred_elemen...  53 us
    all_to_all x1, waiting for transfers between devices, per_device(): lax.all_to_all(tangent_rows, 'uly', split_axis=0, concat_axis=1, tiled=True)  45.8 us
    dot_general x4, matrix products, update(): jnp.einsum('grpqk,kgd->grpqd', weighted.astype(jnp.bfloat16), value_block...  39.9 us
    dot_general x4, matrix products, update(): jnp.einsum('grqk,kgpd->grpqd', weights_half, value_tan, preferred_element...  38.2 us
    dot_general x4, matrix products, update(): jnp.einsum('grqd,kgpd->grpqk', query_heads, key_tan, preferred_element_ty...  36.5 us
    unnamed x9, local copies, waits for them, and re-layouts  21.2 us
    all_gather x1, blocking collectives, per_device(): key_piece = lax.all_gather(head_keys, 'blk', axis=0, tiled=True)  17.9 us
    all_gather x1, blocking collectives, per_device(): value_piece = lax.all_gather(head_values, 'blk', axis=0, tiled=True)  14.7 us
  transfers between devices with their start and end apart: 9, of which 7 were waited for; matrix products, arithmetic and copies ran while one was open for 9% of the time, Pallas kernels for 0%

commit v1 on v0

--- a/solution.py
+++ b/solution.py
@@ -17,6 +17,13 @@
 
 
 def per_device(queries, query_tangents, keys, key_tangents, values, value_tangents, span_order):
+
+    def feed_the_ticks(q_in):
+        return jnp.concatenate(
+            lax.all_to_all(jnp.stack(jnp.split(q_in, lax.axis_size("uly"), axis=0)), "uly", 0, 0),
+            axis=1,
+        )
+
     local_queries, local_tangents = (
         lax.all_to_all(queries, "uly", split_axis=1, concat_axis=0, tiled=True),
         lax.all_to_all(query_tangents, "uly", split_axis=1, concat_axis=0, tiled=True),
@@ -126,7 +133,7 @@
     )
     attention_out, tangent_out = (
         lax.all_to_all(output_rows, "uly", split_axis=0, concat_axis=1, tiled=True),
-        lax.all_to_all(tangent_rows, "uly", split_axis=0, concat_axis=1, tiled=True),
+        feed_the_ticks(tangent_rows),
     )
     return (attention_out, tangent_out)
 

time: 426 us -> 437 us (1.026)
  other arithmetic: 25.2 us -> 31.4 us
    another operation x0 -> x1, other arithmetic: none -> 6.34 us  [feed_the_ticks(): jnp.stack(jnp.split(q_in, lax.axis_size('uly'), axis=0))]
    split x0 -> x5, local copies, waits for them, and re-layouts: none -> 5.45 us  [feed_the_ticks(): jnp.split(q_in, lax.axis_size('uly'), axis=0)]
    transpose x1 -> x0, local copies, waits for them, and re-layouts: 4.71 us -> none  [per_device(): jnp.transpose(tangent.astype(jnp.bfloat16), (3, 0, 1, 2, 4))]
  transfers between devices with their start and end apart: 9 -> 9, of which waited for: 7 -> 7; matrix products, arithmetic and copies ran while one was open for 9% -> 8% of each run, Pallas kernels for 0% -> 0%
where the time goes in v1:
time: 437 us; the launch traced here: 435 us
  matrix products  185 us (42%)
  waiting for transfers between devices  71.4 us (16%)
  local copies, waits for them, and re-layouts  57.4 us (13%)
  blocking collectives  43.3 us (10%)
  other arithmetic  31.4 us (7%)
  starting transfers between devices  26.8 us (6%)
  between operations  14.3 us (3%)
  loops' own time  5.76 us (1%)
    dot_general x4, matrix products, update(): jnp.einsum('grpqd,kgd->grpqk', tangent_heads, key_block, preferred_elemen...  53 us
    all_to_all x1, waiting for transfers between devices, feed_the_ticks(): lax.all_to_all(jnp.stack(jnp.split(q_in, lax.axis_size('uly'), axis=0)),...  45.8 us
    dot_general x4, matrix products, update(): jnp.einsum('grpqk,kgd->grpqd', weighted.astype(jnp.bfloat16), value_block...  39.9 us
    dot_general x4, matrix products, update(): jnp.einsum('grqk,kgpd->grpqd', weights_half, value_tan, preferred_element...  38.2 us
    dot_general x4, matrix products, update(): jnp.einsum('grqd,kgpd->grpqk', query_heads, key_tan, preferred_element_ty...  36.5 us
    unnamed x9, local copies, waits for them, and re-layouts  21.2 us
    all_gather x1, blocking collectives, per_device(): key_piece = lax.all_gather(head_keys, 'blk', axis=0, tiled=True)  17.9 us
    all_gather x1, blocking collectives, per_device(): value_piece = lax.all_gather(head_values, 'blk', axis=0, tiled=True)  14.8 us
  transfers between devices with their start and end apart: 9, of which 7 were waited for; matrix products, arithmetic and copies ran while one was open for 8% of the time, Pallas kernels for 0%

profile of v1, /device:TPU:0, one launch (start us, length us, event | category | flops | bytes accessed | tf_op | source)
XLA Modules:
  0.0 435.5 jit_solution(14963489451604579169)
XLA Ops:
  8.3 10.7 %all_to_all.125 = bf16[32,8,4,128]{3,0,2,1:T(8,128)(2,1)S(1)} all-to-all(bf16[32,8,4,128]{3,0,2,1:T(8,128)(2,1)S(1)} %copy.120), channel_id=1, replica_groups=mesh['blk'=8,'uly'=4] {'uly'}, dimensions={1} | all-to-all | bytes 524288 | tf_op jit(solution)/shard_map/all_to_all | solution.py:101
  21.2 3.3 all-to-all-start
  26.0 3.3 all-to-all-done
  29.3 3.3 all-to-all-start.2
  34.4 3.1 all-to-all-done.2
  37.4 3.4 all-to-all-start.5
  46.2 3.5 all-to-all-start.1
  50.5 6.6 %copy.118 = bf16[32,128,4,128]{3,2,0,1:T(4,128)(2,1)} copy(bf16[32,128,4,128]{3,2,1,0:T(4,128)(2,1)} %param.12) | data formatting | bytes 8388608 | tf_op args[1]
  59.7 4.9 %all-to-all-start.3 = ((bf16[32,128,4,128]{3,2,0,1:T(4,128)(2,1)}), bf16[32,128,4,128]{3,2,0,1:T(4,128)(2,1)}, u32[]{:S(2)}, u32[]{:S(2)}) async-start(bf16[32,128,4,128]{3,2,0,1:T(4,128)(2,1)} %copy.118), calls=%async_computation.3 | async-start | bytes 8388608 | tf_op jit(solution)/shard_map/all_to_all | solution.py:29
  65.5 17.9 %all_gather.12 = bf16[1024,2,128]{2,0,1:T(8,128)(2,1)S(1)} all-gather(bf16[128,2,128]{2,0,1:T(8,128)(2,1)S(1)} %bitcast.144), channel_id=1, replica_groups=mesh['blk'=8,'uly'=4] {'blk'}, dimensions={0}, use_global_device_ids=true | all-gather | bytes 589824 | tf_op jit(solution)/shard_map/all_gather | solution.py:106
  84.3 14.8 %all_gather.13 = bf16[1024,2,128]{2,0,1:T(8,128)(2,1)S(1)} all-gather(bf16[128,2,128]{2,0,1:T(8,128)(2,1)S(1)} %bitcast.145), channel_id=1, replica_groups=mesh['blk'=8,'uly'=4] {'blk'}, dimensions={0}, use_global_device_ids=true | all-gather | bytes 589824 | tf_op jit(solution)/shard_map/all_gather | solution.py:108
  100.0 7.4 %all-to-all-done.3 = bf16[32,128,4,128]{3,2,0,1:T(4,128)(2,1)} async-done(((bf16[32,128,4,128]{3,2,0,1:T(4,128)(2,1)}), bf16[32,128,4,128]{3,2,0,1:T(4,128)(2,1)}, u32[]{:S(2)}, u32[]{:S(2)}) %all-to-all-start.3) | async-done | bytes 4194336 | tf_op jit(solution)/shard_map/all_to_all | solution.py:29
  107.4 5.4 %copy.119 = bf16[4,32,32,4,128]{4,1,0,3,2:T(8,128)(2,1)} copy(bf16[4,32,32,4,128]{4,3,1,2,0:T(4,128)(2,1)} %bitcast.37) | data formatting | bytes 8388608 | tf_op jit(solution)/shard_map/all_to_all | solution.py:29
  112.8 3.1 copy.126
  117.6 4.3 broadcast_in_dim.87
  123.5 212.6 %while.18 = (s32[]{:T(128)}, f32[2,16,128]{2,1,0:T(8,128)S(1)}, f32[2,16,128]{2,1,0:T(8,128)S(1)}, f32[2,16,128,128]{3,2,1,0:T(8,128)}, f32[2,16,4,128,128]{4,3,...) while((s32[]{:T(128)}, f32[2,16,128]{2,1,0:T(8,128)S(1)}, ...), condition=%wide.region_10.11_spmd, body=%wide.region_3.10_spmd.sunk | while | flops 4875936256 | bytes 138631600 | solution.py:121
  125.7 51.2 %conditional.2 = ((f32[2,16,128]{2,1,0:T(8,128)S(1)}, f32[2,16,128]{2,1,0:T(8,128)S(1)}, f32[2,16,128,128]{3,2,1,0:T(8,128)}, f32[2,16,4,128,128]{4,3,2,1,0:T(8,128)}, f32[2,16,4,128]{3,2,1,0:T(4,128)S(1)})) conditional(s32[]{:T(128)} %convert_element_type.33, (f32[2,16,128]{2,1,0:T(8,128)S(1)}, f32[2,16,128]{2,1,0:T(8,128)S(1)}, ...), branch_computations={%region_5.5_spmd, %region_6.9_spmd} | conditional | flops 4875935744 | bytes 138629216 | solution.py:90
  127.5 3.3 broadcast_multiply_fusion
  130.8 9.1 %fusion.7 = f32[2,256,4,16,128]{4,1,2,3,0:T(8,128)} fusion(bf16[2,16,128,128]{3,2,1,0:T(8,128)(2,1)S(1)} %get-tuple-element.183, bf16[4,256,2,4,128]{4,1,3,2,0:T(8,128)(2,1)} %get-tuple-element.189, s32[]{:T(128)} %get-tuple-element.182), kind=kOutput, calls=%fused_computation.13 | convolution fusion | flops 1073741824 | bytes 18350592 | tf_op jit(solution)/shard_map/while/body/eval_jaxpr/cond/branch_1_fun/grqd,kgpd->grpqk/dot_general | solution.py:64
  139.9 13.3 %fusion.40 = (f32[2,16,4,128]{3,2,1,0:T(4,128)S(1)}, bf16[2,16,4,128,256]{3,4,2,1,0:T(8,128)(2,1)}) fusion(f32[2,16,128,256]{2,3,1,0:T(8,128)} %get-tuple-element.340, f32[2,256,4,16,128]{4,1,2,3,0:T(8,128)} %fusion.7, bf16[2,16,4,128,128]{4,3,2,1,0:T(8,128)(2,1)} %get-tuple-element.188, bf16[4,256,2,128]{3,1,2,0:T(8,128)(2,1)} %get-tuple-element.181, ...), kind=kOutput, calls=%fused_computation.71 | convolution fusion | flops 1090502656 | bytes 33751552 | tf_op jit(solution)/shard_map/while/body/eval_jaxpr/cond/branch_1_fun/grpqd,kgd->grpqk/dot_general | solution.py:61
  153.2 10.0 %fusion.1 = f32[2,16,4,128,128]{4,3,2,1,0:T(8,128)} fusion(bf16[2,16,4,128,256]{3,4,2,1,0:T(8,128)(2,1)} %get-tuple-element.345, bf16[4,256,2,128]{3,1,2,0:T(8,128)(2,1)} %get-tuple-element.186, s32[]{:T(128)} %get-tuple-element.182), kind=kOutput, calls=%fused_computation.3 | convolution fusion | flops 1073741824 | bytes 16908800 | tf_op jit(solution)/shard_map/while/body/eval_jaxpr/cond/branch_1_fun/grpqk,kgd->grpqd/dot_general | solution.py:74
  163.2 9.5 %bitcast_add_fusion.1 = f32[2,16,4,128,128]{4,3,2,1,0:T(8,128)} fusion(f32[2,16,4,128,128]{4,3,2,1,0:T(8,128)} %fusion.1, f32[2,16,4,128,128]{4,3,2,1,0:T(8,128)} %get-tuple-element.187, f32[2,16,128]{2,1,0:T(8,128)S(1)} %get-tuple-element.333, bf16[4,256,2,4,128]{4,1,3,2,0:T(8,128)(2,1)S(1)} %get-tuple-element.190, s32[]{:T(128)} %get-tuple-element.182, ...), kind=kOutput, calls=%fused_computation.2 | convolution fusion | flops 1085276160 | bytes 29949956 | tf_op jit(solution)/shard_map/while/body/eval_jaxpr/cond/branch_1_fun/grqk,kgpd->grpqd/dot_general | solution.py:80
  178.8 51.2 %conditional.2 = ((f32[2,16,128]{2,1,0:T(8,128)S(1)}, f32[2,16,128]{2,1,0:T(8,128)S(1)}, f32[2,16,128,128]{3,2,1,0:T(8,128)}, f32[2,16,4,128,128]{4,3,2,1,0:T(8,128)}, f32[2,16,4,128]{3,2,1,0:T(4,128)S(1)})) conditional(s32[]{:T(128)} %convert_element_type.33, (f32[2,16,128]{2,1,0:T(8,128)S(1)}, f32[2,16,128]{2,1,0:T(8,128)S(1)}, ...), branch_computations={%region_5.5_spmd, %region_6.9_spmd} | conditional | flops 4875935744 | bytes 138629216 | solution.py:90
  180.6 3.3 broadcast_multiply_fusion
  183.9 9.1 %fusion.7 = f32[2,256,4,16,128]{4,1,2,3,0:T(8,128)} fusion(bf16[2,16,128,128]{3,2,1,0:T(8,128)(2,1)S(1)} %get-tuple-element.183, bf16[4,256,2,4,128]{4,1,3,2,0:T(8,128)(2,1)} %get-tuple-element.189, s32[]{:T(128)} %get-tuple-element.182), kind=kOutput, calls=%fused_computation.13 | convolution fusion | flops 1073741824 | bytes 18350592 | tf_op jit(solution)/shard_map/while/body/eval_jaxpr/cond/branch_1_fun/grqd,kgpd->grpqk/dot_general | solution.py:64
  193.0 13.3 %fusion.40 = (f32[2,16,4,128]{3,2,1,0:T(4,128)S(1)}, bf16[2,16,4,128,256]{3,4,2,1,0:T(8,128)(2,1)}) fusion(f32[2,16,128,256]{2,3,1,0:T(8,128)} %get-tuple-element.340, f32[2,256,4,16,128]{4,1,2,3,0:T(8,128)} %fusion.7, bf16[2,16,4,128,128]{4,3,2,1,0:T(8,128)(2,1)} %get-tuple-element.188, bf16[4,256,2,128]{3,1,2,0:T(8,128)(2,1)} %get-tuple-element.181, ...), kind=kOutput, calls=%fused_computation.71 | convolution fusion | flops 1090502656 | bytes 33751552 | tf_op jit(solution)/shard_map/while/body/eval_jaxpr/cond/branch_1_fun/grpqd,kgd->grpqk/dot_general | solution.py:61
  206.3 10.0 %fusion.1 = f32[2,16,4,128,128]{4,3,2,1,0:T(8,128)} fusion(bf16[2,16,4,128,256]{3,4,2,1,0:T(8,128)(2,1)} %get-tuple-element.345, bf16[4,256,2,128]{3,1,2,0:T(8,128)(2,1)} %get-tuple-element.186, s32[]{:T(128)} %get-tuple-element.182), kind=kOutput, calls=%fused_computation.3 | convolution fusion | flops 1073741824 | bytes 16908800 | tf_op jit(solution)/shard_map/while/body/eval_jaxpr/cond/branch_1_fun/grpqk,kgd->grpqd/dot_general | solution.py:74
  216.3 9.5 %bitcast_add_fusion.1 = f32[2,16,4,128,128]{4,3,2,1,0:T(8,128)} fusion(f32[2,16,4,128,128]{4,3,2,1,0:T(8,128)} %fusion.1, f32[2,16,4,128,128]{4,3,2,1,0:T(8,128)} %get-tuple-element.187, f32[2,16,128]{2,1,0:T(8,128)S(1)} %get-tuple-element.333, bf16[4,256,2,4,128]{4,1,3,2,0:T(8,128)(2,1)S(1)} %get-tuple-element.190, s32[]{:T(128)} %get-tuple-element.182, ...), kind=kOutput, calls=%fused_computation.2 | convolution fusion | flops 1085276160 | bytes 29949956 | tf_op jit(solution)/shard_map/while/body/eval_jaxpr/cond/branch_1_fun/grqk,kgpd->grpqd/dot_general | solution.py:80
  231.9 51.2 %conditional.2 = ((f32[2,16,128]{2,1,0:T(8,128)S(1)}, f32[2,16,128]{2,1,0:T(8,128)S(1)}, f32[2,16,128,128]{3,2,1,0:T(8,128)}, f32[2,16,4,128,128]{4,3,2,1,0:T(8,128)}, f32[2,16,4,128]{3,2,1,0:T(4,128)S(1)})) conditional(s32[]{:T(128)} %convert_element_type.33, (f32[2,16,128]{2,1,0:T(8,128)S(1)}, f32[2,16,128]{2,1,0:T(8,128)S(1)}, ...), branch_computations={%region_5.5_spmd, %region_6.9_spmd} | conditional | flops 4875935744 | bytes 138629216 | solution.py:90
  233.7 3.3 broadcast_multiply_fusion
  237.0 9.1 %fusion.7 = f32[2,256,4,16,128]{4,1,2,3,0:T(8,128)} fusion(bf16[2,16,128,128]{3,2,1,0:T(8,128)(2,1)S(1)} %get-tuple-element.183, bf16[4,256,2,4,128]{4,1,3,2,0:T(8,128)(2,1)} %get-tuple-element.189, s32[]{:T(128)} %get-tuple-element.182), kind=kOutput, calls=%fused_computation.13 | convolution fusion | flops 1073741824 | bytes 18350592 | tf_op jit(solution)/shard_map/while/body/eval_jaxpr/cond/branch_1_fun/grqd,kgpd->grpqk/dot_general | solution.py:64
  246.1 13.3 %fusion.40 = (f32[2,16,4,128]{3,2,1,0:T(4,128)S(1)}, bf16[2,16,4,128,256]{3,4,2,1,0:T(8,128)(2,1)}) fusion(f32[2,16,128,256]{2,3,1,0:T(8,128)} %get-tuple-element.340, f32[2,256,4,16,128]{4,1,2,3,0:T(8,128)} %fusion.7, bf16[2,16,4,128,128]{4,3,2,1,0:T(8,128)(2,1)} %get-tuple-element.188, bf16[4,256,2,128]{3,1,2,0:T(8,128)(2,1)} %get-tuple-element.181, ...), kind=kOutput, calls=%fused_computation.71 | convolution fusion | flops 1090502656 | bytes 33751552 | tf_op jit(solution)/shard_map/while/body/eval_jaxpr/cond/branch_1_fun/grpqd,kgd->grpqk/dot_general | solution.py:61
  259.4 10.0 %fusion.1 = f32[2,16,4,128,128]{4,3,2,1,0:T(8,128)} fusion(bf16[2,16,4,128,256]{3,4,2,1,0:T(8,128)(2,1)} %get-tuple-element.345, bf16[4,256,2,128]{3,1,2,0:T(8,128)(2,1)} %get-tuple-element.186, s32[]{:T(128)} %get-tuple-element.182), kind=kOutput, calls=%fused_computation.3 | convolution fusion | flops 1073741824 | bytes 16908800 | tf_op jit(solution)/shard_map/while/body/eval_jaxpr/cond/branch_1_fun/grpqk,kgd->grpqd/dot_general | solution.py:74
  269.4 9.5 %bitcast_add_fusion.1 = f32[2,16,4,128,128]{4,3,2,1,0:T(8,128)} fusion(f32[2,16,4,128,128]{4,3,2,1,0:T(8,128)} %fusion.1, f32[2,16,4,128,128]{4,3,2,1,0:T(8,128)} %get-tuple-element.187, f32[2,16,128]{2,1,0:T(8,128)S(1)} %get-tuple-element.333, bf16[4,256,2,4,128]{4,1,3,2,0:T(8,128)(2,1)S(1)} %get-tuple-element.190, s32[]{:T(128)} %get-tuple-element.182, ...), kind=kOutput, calls=%fused_computation.2 | convolution fusion | flops 1085276160 | bytes 29949956 | tf_op jit(solution)/shard_map/while/body/eval_jaxpr/cond/branch_1_fun/grqk,kgpd->grpqd/dot_general | solution.py:80
  285.0 51.2 %conditional.2 = ((f32[2,16,128]{2,1,0:T(8,128)S(1)}, f32[2,16,128]{2,1,0:T(8,128)S(1)}, f32[2,16,128,128]{3,2,1,0:T(8,128)}, f32[2,16,4,128,128]{4,3,2,1,0:T(8,128)}, f32[2,16,4,128]{3,2,1,0:T(4,128)S(1)})) conditional(s32[]{:T(128)} %convert_element_type.33, (f32[2,16,128]{2,1,0:T(8,128)S(1)}, f32[2,16,128]{2,1,0:T(8,128)S(1)}, ...), branch_computations={%region_5.5_spmd, %region_6.9_spmd} | conditional | flops 4875935744 | bytes 138629216 | solution.py:90
  286.8 3.3 broadcast_multiply_fusion
  290.1 9.1 %fusion.7 = f32[2,256,4,16,128]{4,1,2,3,0:T(8,128)} fusion(bf16[2,16,128,128]{3,2,1,0:T(8,128)(2,1)S(1)} %get-tuple-element.183, bf16[4,256,2,4,128]{4,1,3,2,0:T(8,128)(2,1)} %get-tuple-element.189, s32[]{:T(128)} %get-tuple-element.182), kind=kOutput, calls=%fused_computation.13 | convolution fusion | flops 1073741824 | bytes 18350592 | tf_op jit(solution)/shard_map/while/body/eval_jaxpr/cond/branch_1_fun/grqd,kgpd->grpqk/dot_general | solution.py:64
  299.2 13.3 %fusion.40 = (f32[2,16,4,128]{3,2,1,0:T(4,128)S(1)}, bf16[2,16,4,128,256]{3,4,2,1,0:T(8,128)(2,1)}) fusion(f32[2,16,128,256]{2,3,1,0:T(8,128)} %get-tuple-element.340, f32[2,256,4,16,128]{4,1,2,3,0:T(8,128)} %fusion.7, bf16[2,16,4,128,128]{4,3,2,1,0:T(8,128)(2,1)} %get-tuple-element.188, bf16[4,256,2,128]{3,1,2,0:T(8,128)(2,1)} %get-tuple-element.181, ...), kind=kOutput, calls=%fused_computation.71 | convolution fusion | flops 1090502656 | bytes 33751552 | tf_op jit(solution)/shard_map/while/body/eval_jaxpr/cond/branch_1_fun/grpqd,kgd->grpqk/dot_general | solution.py:61
  312.5 10.0 %fusion.1 = f32[2,16,4,128,128]{4,3,2,1,0:T(8,128)} fusion(bf16[2,16,4,128,256]{3,4,2,1,0:T(8,128)(2,1)} %get-tuple-element.345, bf16[4,256,2,128]{3,1,2,0:T(8,128)(2,1)} %get-tuple-element.186, s32[]{:T(128)} %get-tuple-element.182), kind=kOutput, calls=%fused_computation.3 | convolution fusion | flops 1073741824 | bytes 16908800 | tf_op jit(solution)/shard_map/while/body/eval_jaxpr/cond/branch_1_fun/grpqk,kgd->grpqd/dot_general | solution.py:74
  322.5 9.5 %bitcast_add_fusion.1 = f32[2,16,4,128,128]{4,3,2,1,0:T(8,128)} fusion(f32[2,16,4,128,128]{4,3,2,1,0:T(8,128)} %fusion.1, f32[2,16,4,128,128]{4,3,2,1,0:T(8,128)} %get-tuple-element.187, f32[2,16,128]{2,1,0:T(8,128)S(1)} %get-tuple-element.333, bf16[4,256,2,4,128]{4,1,3,2,0:T(8,128)(2,1)S(1)} %get-tuple-element.190, s32[]{:T(128)} %get-tuple-element.182, ...), kind=kOutput, calls=%fused_computation.2 | convolution fusion | flops 1085276160 | bytes 29949956 | tf_op jit(solution)/shard_map/while/body/eval_jaxpr/cond/branch_1_fun/grqk,kgpd->grpqd/dot_general | solution.py:80
  338.1 5.7 %fusion.30 = bf16[128,2,16,4,128]{4,0,3,2,1:T(8,128)(2,1)S(1)} fusion(f32[2,16,4,128]{3,2,1,0:T(4,128)S(1)} %broadcast_divide_fusion.1, f32[2,16,128,128]{3,2,1,0:T(8,128)S(1)} %get-tuple-element.337, f32[2,16,4,128,128]{4,3,2,1,0:T(8,128)} %get-tuple-element.221, f32[2,16,128]{2,1,0:T(8,128)S(1)} %get-tuple-element.220), kind=kLoop, calls=%fused_computation.41 | loop fusion | flops 8388608 | bytes 14761984 | tf_op jit(solution)/shard_map/transpose | solution.py:131
  350.9 3.5 all-to-all-start.6
  354.4 6.3 %pad_maximum_fusion = bf16[4,32,32,4,128]{4,3,2,1,0:T(4,128)(2,1)} fusion(bf16[1,32,32,4,128]{4,3,2,1,0:T(4,128)(2,1)} %bitcast.134, bf16[1,32,32,4,128]{4,3,2,1,0:T(4,128)(2,1)} %bitcast.133, bf16[1,32,32,4,128]{4,3,2,1,0:T(4,128)(2,1)S(1)} %bitcast.132, bf16[1,32,32,4,128]{4,3,2,1,0:T(4,128)(2,1)S(1)} %bitcast.131), kind=kLoop, calls=%fused_computation.40 | loop fusion | flops 6291456 | bytes 8388608 | tf_op jit(solution)/shard_map/stack | solution.py:23
  360.8 6.8 %all-to-all-done.6 = bf16[128,32,128]{2,1,0:T(8,128)(2,1)S(1)} async-done(((bf16[128,32,128]{2,1,0:T(8,128)(2,1)}), bf16[128,32,128]{2,1,0:T(8,128)(2,1)S(1)}, u32[]{:S(2)}, u32[]{:S(2)}) %all-to-all-start.6) | async-done | bytes 1048608 | tf_op jit(solution)/shard_map/all_to_all | solution.py:135
  367.6 4.9 %all-to-all-start.7 = ((bf16[4,32,32,4,128]{4,3,2,1,0:T(4,128)(2,1)}), bf16[4,32,32,4,128]{4,3,2,1,0:T(4,128)(2,1)}, u32[]{:S(2)}, u32[]{:S(2)}) async-start(bf16[4,32,32,4,128]{4,3,2,1,0:T(4,128)(2,1)} %pad_maximum_fusion), calls=%async_computation.7 | async-start | bytes 8388608 | tf_op jit(solution)/shard_map/all_to_all | solution.py:23
  373.5 45.8 %all-to-all-done.7 = bf16[4,32,32,4,128]{4,3,2,1,0:T(4,128)(2,1)} async-done(((bf16[4,32,32,4,128]{4,3,2,1,0:T(4,128)(2,1)}), bf16[4,32,32,4,128]{4,3,2,1,0:T(4,128)(2,1)}, u32[]{:S(2)}, u32[]{:S(2)}) %all-to-all-start.7) | async-done | bytes 4194336 | tf_op jit(solution)/shard_map/all_to_all | solution.py:23
  419.3 3.3 copy.134
  422.7 5.9 %copy.135 = bf16[32,128,4,128]{3,2,1,0:T(4,128)(2,1)} copy(bf16[32,128,4,128]{3,1,2,0:T(8,128)(2,1)S(1)} %bitcast.128) | data formatting | bytes 8388608
  (92 shorter events, 57.5 us)
Async XLA Ops:
  7.2 105.6 %all-gather.3.cloned.1.call-start = ((), (), s32[]{:S(2)}) async-start(), calls=%async_computation.8 | async-start | bytes 2359296 | tf_op jit(solution)/shard_map/all_gather | solution.py:107
  21.2 8.1 %all-to-all-start = ((bf16[32,8,128]{2,0,1:T(8,128)(2,1)}), bf16[32,8,128]{2,0,1:T(8,128)(2,1)S(1)}, u32[]{:S(2)}, u32[]{:S(2)}) async-start(bf16[32,8,128]{2,0,1:T(8,128)(2,1)} %copy.112), calls=%async_computation | async-start | bytes 131072 | tf_op jit(solution)/shard_map/all_to_all | solution.py:100
  29.3 8.1 %all-to-all-start.2 = ((bf16[32,8,128]{2,0,1:T(8,128)(2,1)}), bf16[32,8,128]{2,0,1:T(8,128)(2,1)S(1)}, u32[]{:S(2)}, u32[]{:S(2)}) async-start(bf16[32,8,128]{2,0,1:T(8,128)(2,1)} %copy.116), calls=%async_computation.2 | async-start | bytes 131072 | tf_op jit(solution)/shard_map/all_to_all | solution.py:102
  37.4 8.8 %all-to-all-start.5 = ((bf16[32,8,4,128]{3,0,2,1:T(8,128)(2,1)}), bf16[32,8,4,128]{3,0,2,1:T(8,128)(2,1)S(1)}, u32[]{:S(2)}, u32[]{:S(2)}) async-start(bf16[32,8,4,128]{3,0,2,1:T(8,128)(2,1)} %copy.122), calls=%async_computation.5 | async-start | bytes 524288 | tf_op jit(solution)/shard_map/all_to_all | solution.py:103
  46.2 13.5 %all-to-all-start.1 = ((bf16[32,128,128]{2,0,1:T(8,128)(2,1)}), bf16[32,128,128]{2,0,1:T(8,128)(2,1)S(1)}, u32[]{:S(2)}, u32[]{:S(2)}) async-start(bf16[32,128,128]{2,0,1:T(8,128)(2,1)} %copy.114), calls=%async_computation.1 | async-start | bytes 2097152 | tf_op jit(solution)/shard_map/all_to_all | solution.py:28
  49.7 66.2 %all-gather.5.cloned.1.call-start = ((), (), s32[]{:S(2)}) async-start(), calls=%async_computation.9 | async-start | bytes 2359296 | tf_op jit(solution)/shard_map/all_gather | solution.py:109
  57.1 7.5 %copy-start.2 = (s32[16]{0:T(128)S(1)}, s32[16]{0:T(128)}, u32[]{:S(2)}) copy-start(s32[16]{0:T(128)} %param.17) | copy-start | bytes 196
  59.7 47.7 %all-to-all-start.3 = ((bf16[32,128,4,128]{3,2,0,1:T(4,128)(2,1)}), bf16[32,128,4,128]{3,2,0,1:T(4,128)(2,1)}, u32[]{:S(2)}, u32[]{:S(2)}) async-start(bf16[32,128,4,128]{3,2,0,1:T(4,128)(2,1)} %copy.118), calls=%async_computation.3 | async-start | bytes 8388608 | tf_op jit(solution)/shard_map/all_to_all | solution.py:29
  163.1 9.6 %copy-start = (f32[2,16,128,128]{3,2,1,0:T(8,128)S(1)}, f32[2,16,128,128]{3,2,1,0:T(8,128)}, u32[]{:S(2)}) copy-start(f32[2,16,128,128]{3,2,1,0:T(8,128)} %get-tuple-element.185) | copy-start | bytes 6291460 | tf_op jit(solution)/shard_map/while/body/eval_jaxpr/cond
  175.5 1.3 copy-start.1
  216.3 9.6 %copy-start = (f32[2,16,128,128]{3,2,1,0:T(8,128)S(1)}, f32[2,16,128,128]{3,2,1,0:T(8,128)}, u32[]{:S(2)}) copy-start(f32[2,16,128,128]{3,2,1,0:T(8,128)} %get-tuple-element.185) | copy-start | bytes 6291460 | tf_op jit(solution)/shard_map/while/body/eval_jaxpr/cond
  228.6 1.3 copy-start.1
  269.4 9.6 %copy-start = (f32[2,16,128,128]{3,2,1,0:T(8,128)S(1)}, f32[2,16,128,128]{3,2,1,0:T(8,128)}, u32[]{:S(2)}) copy-start(f32[2,16,128,128]{3,2,1,0:T(8,128)} %get-tuple-element.185) | copy-start | bytes 6291460 | tf_op jit(solution)/shard_map/while/body/eval_jaxpr/cond
  281.7 1.3 copy-start.1
  322.5 9.6 %copy-start = (f32[2,16,128,128]{3,2,1,0:T(8,128)S(1)}, f32[2,16,128,128]{3,2,1,0:T(8,128)}, u32[]{:S(2)}) copy-start(f32[2,16,128,128]{3,2,1,0:T(8,128)} %get-tuple-element.185) | copy-start | bytes 6291460 | tf_op jit(solution)/shard_map/while/body/eval_jaxpr/cond
  334.8 1.3 copy-start.1
  350.9 16.6 %all-to-all-start.6 = ((bf16[128,32,128]{2,1,0:T(8,128)(2,1)}), bf16[128,32,128]{2,1,0:T(8,128)(2,1)S(1)}, u32[]{:S(2)}, u32[]{:S(2)}) async-start(bf16[128,32,128]{2,1,0:T(8,128)(2,1)} %bitcast.49), calls=%async_computation.6 | async-start | bytes 2097152 | tf_op jit(solution)/shard_map/all_to_all | solution.py:135
  367.6 51.8 %all-to-all-start.7 = ((bf16[4,32,32,4,128]{4,3,2,1,0:T(4,128)(2,1)}), bf16[4,32,32,4,128]{4,3,2,1,0:T(4,128)(2,1)}, u32[]{:S(2)}, u32[]{:S(2)}) async-start(bf16[4,32,32,4,128]{4,3,2,1,0:T(4,128)(2,1)} %pad_maximum_fusion), calls=%async_computation.7 | async-start | bytes 8388608 | tf_op jit(solution)/shard_map/all_to_all | solution.py:23
Sparse Core Ops, SparseCore 0:
  19.9 28.8 all-gather.2
  52.1 35.0 all-gather.4
